TPU v7x, 32 devices: a whole 2x2x4 slice. The times are simulated.
32 devices in a mesh: groups: 2 (over x), mp: 16 (over z, y, core).
Axes of the slice: x: 2, y: 2, z: 4, core: 2. Of those that a mesh axis runs over, the one named last changes fastest.
Arguments:
- tokens: bfloat16 [512, 8192], P(('groups', 'mp')), parts along dimension 0, may hold values from -6 to 6
- queries: bfloat16 [512, 8192], P(('groups', 'mp')), parts along dimension 0, may hold values from -35 to 35
- key_proj: bfloat16 [512, 1024], P(('groups', 'mp')), parts along dimension 0, may hold values from -5 to 5
- values: bfloat16 [512, 1024], P(('groups', 'mp')), parts along dimension 0, may hold values from -6 to 6
- seq_lens: int32 [12], P('groups'), parts along dimension 0, may hold values from 21 to 85, as said below
- out_weight: bfloat16 [8192, 8192], P('mp'), may hold values from -0.25 to 0.25
- ffn_gain: float32 [2, 8192], replicated, may hold values from 0.25 to 2.5
- gate_weight: bfloat16 [8192, 12288], P(None, 'mp'), may hold values from -0.0625 to 0.0625
- up_weight: bfloat16 [8192, 12288], P(None, 'mp'), may hold values from -0.0625 to 0.0625
- down_weight: bfloat16 [12288, 8192], P('mp'), may hold values from -0.0546875 to 0.0546875
- slice_table: int32 [96], replicated, may hold values from 0 to 1, as said below
Outputs:
- stream: bfloat16 [512, 8192], P(('groups', 'mp')), parts along dimension 0
- mixed: bfloat16 [512, 8192], P(('groups', 'mp')), parts along dimension 0
There are 2 independent parts, one for each index of `groups`. A program takes and returns all parts, laid end to end along the dimension named above; an argument that names none is the same for every part. Nothing has to cross between parts.
Inputs may be any that keep to these rules, and one draw needn't show every extreme that they name: `seq_lens`: the 6 lengths sum to 256; the shortest is exactly 21 and the longest exactly 85. `slice_table`: exactly 16 entries are 1, the rest 0.
All inputs are finite; a program needn't handle non-finite values.
Results may differ from a plain program's by a relative error of at most 0.02.
Values may be sent and summed in bfloat16 or wider, within the bound.
A program may use at most 128 MiB of HBM per device.

v0:
```python
import math

import jax
import jax.numpy as jnp
from jax import lax
from jax.sharding import PartitionSpec as P

QUERY_HEADS = 64
HEAD_SIZE = 128
SLICE = 128


def segment_of(positions, seq_ends):
    return jnp.sum((positions[:, None] >= seq_ends[None, :]).astype(jnp.int32), axis=1)


def allowed(query_pos, key_pos, seq_ends):
    query_seg = segment_of(query_pos, seq_ends)
    key_seg = segment_of(key_pos, seq_ends)
    return (query_seg[:, None] == key_seg[None, :]) & (key_pos[None, :] <= query_pos[:, None])


def soft_weights(scores, visible):
    masked = jnp.where(visible, scores, -1e30)
    highest = jnp.max(masked, axis=-1, keepdims=True)
    expo = jnp.where(visible, jnp.exp(masked - highest), 0.0)
    return (expo / jnp.sum(expo, axis=-1, keepdims=True)).astype(jnp.bfloat16)


def rms_normed(stream_rows):
    stream_full = stream_rows.astype(jnp.float32)
    inv_rms = lax.rsqrt(jnp.mean(stream_full * stream_full, axis=1, keepdims=True) + 1e-05)
    return (stream_full * inv_rms).astype(jnp.bfloat16)


def local(
    tokens,
    queries,
    key_proj,
    values,
    seq_lens,
    out_weight,
    ffn_gain,
    gate_weight,
    up_weight,
    down_weight,
    slice_table,
):
    tok_dev = tokens.shape[0]
    my_index = lax.axis_index("mp")
    token_count = tok_dev * lax.axis_size("mp")
    heads_kv = key_proj.shape[1] // HEAD_SIZE
    query_heads_per_group = QUERY_HEADS // heads_kv
    score_scale = 1.0 / math.sqrt(HEAD_SIZE)
    key_all, value_all = (
        lax.all_gather(key_proj, "mp", axis=0, tiled=True),
        lax.all_gather(values, "mp", axis=0, tiled=True),
    )
    seq_ends = jnp.cumsum(seq_lens)
    key_pos = jnp.arange(token_count, dtype=jnp.int32)
    query_heads = lax.all_to_all(queries, "mp", split_axis=1, concat_axis=0, tiled=True)
    local_heads = query_heads.shape[1] // HEAD_SIZE
    kv_start = my_index * local_heads // query_heads_per_group * HEAD_SIZE
    key_cols = lax.dynamic_slice_in_dim(key_all, kv_start, HEAD_SIZE, 1)
    value_cols = lax.dynamic_slice_in_dim(value_all, kv_start, HEAD_SIZE, 1)
    visible = allowed(key_pos, key_pos, seq_ends)
    scores = (
        jnp.einsum(
            "thd,sd->hts",
            query_heads.reshape(token_count, local_heads, HEAD_SIZE),
            key_cols,
            preferred_element_type=jnp.float32,
        )
        * score_scale
    )
    attn_probs = soft_weights(scores, visible[None])
    context = (
        jnp.einsum("hts,sd->thd", attn_probs, value_cols, preferred_element_type=jnp.float32)
        .astype(jnp.bfloat16)
        .reshape(token_count, local_heads * HEAD_SIZE)
    )
    picked = context
    attn_share = lax.psum_scatter(
        jnp.dot(picked, out_weight, preferred_element_type=jnp.float32).astype(jnp.bfloat16),
        "mp",
        scatter_dimension=0,
        tiled=True,
    ).astype(jnp.float32)
    stream = (tokens.astype(jnp.float32) + attn_share).astype(jnp.bfloat16)
    sent_rows = rms_normed(stream)
    slice_count = gate_weight.shape[1] // SLICE
    row_piece = lax.all_gather(sent_rows, "mp", axis=0, tiled=True)
    outputs = []
    for slice_pos in range(slice_count):
        ffn_which = lax.dynamic_index_in_dim(
            slice_table, my_index * slice_count + slice_pos, 0, keepdims=False
        )
        gain_row = lax.dynamic_index_in_dim(ffn_gain, ffn_which, 0, keepdims=False)
        slice_input = (row_piece.astype(jnp.float32) * gain_row[None, :]).astype(jnp.bfloat16)
        gate_val = jnp.dot(
            slice_input,
            gate_weight[:, slice_pos * SLICE : (slice_pos + 1) * SLICE],
            preferred_element_type=jnp.float32,
        )
        up_val = jnp.dot(
            slice_input,
            up_weight[:, slice_pos * SLICE : (slice_pos + 1) * SLICE],
            preferred_element_type=jnp.float32,
        )
        outputs.append((jax.nn.silu(gate_val) * up_val).astype(jnp.bfloat16))
    hidden = jnp.concatenate(outputs, axis=1)
    picked = hidden
    ffn_share = lax.psum_scatter(
        jnp.dot(picked, down_weight, preferred_element_type=jnp.float32).astype(jnp.bfloat16),
        "mp",
        scatter_dimension=0,
        tiled=True,
    ).astype(jnp.float32)
    mixed = (stream.astype(jnp.float32) + ffn_share).astype(jnp.bfloat16)
    return (stream, mixed)


def solution(mesh):
    placed = (
        P(("groups", "mp"), None),
        P(("groups", "mp"), None),
        P(("groups", "mp"), None),
        P(("groups", "mp"), None),
        P("groups"),
        P("mp", None),
        P(),
        P(None, "mp"),
        P(None, "mp"),
        P("mp", None),
        P(),
    )
    return jax.shard_map(
        local,
        mesh=mesh,
        in_specs=placed,
        out_specs=(P(("groups", "mp"), None), P(("groups", "mp"), None)),
        check_vma=False,
    )
```

profile of v0, /device:TPU:0, one launch (start us, length us, event | category | flops | bytes accessed | tf_op | source)
XLA Modules:
  0.0 304.8 jit_solution(16253626223594990531)
XLA Ops:
  7.2 1.7 copy.43
  8.8 7.4 %all-to-all-start = ((bf16[16,16,512]{2,0,1:T(8,128)(2,1)}), bf16[16,16,512]{2,0,1:T(8,128)(2,1)S(1)}, u32[]{:S(2)}, u32[]{:S(2)}) async-start(bf16[16,16,512]{2,0,1:T(8,128)(2,1)} %bitcast.57), calls=%async_computation | async-start | bytes 524288 | tf_op jit(solution)/shard_map/all_to_all | solution.py:61
  17.3 23.5 %all_gather.10 = bf16[256,1024]{1,0:T(8,128)(2,1)S(1)} all-gather(bf16[16,1024]{1,0:T(8,128)(2,1)} %param.13), channel_id=1, replica_groups=mesh['groups'=2,'mp'=16] {'mp'}, dimensions={0}, use_global_device_ids=true | all-gather | bytes 557056 | tf_op jit(solution)/shard_map/all_gather | solution.py:56
  40.8 19.1 %all_gather.9 = bf16[256,1024]{1,0:T(8,128)(2,1)S(1)} all-gather(bf16[16,1024]{1,0:T(8,128)(2,1)} %param.14), channel_id=1, replica_groups=mesh['groups'=2,'mp'=16] {'mp'}, dimensions={0}, use_global_device_ids=true | all-gather | bytes 557056 | tf_op jit(solution)/shard_map/all_gather | solution.py:57
  61.4 7.7 %convolution_convert_fusion = bf16[256,8192]{1,0:T(8,128)(2,1)} fusion(bf16[256,512]{0,1:T(8,128)(2,1)S(1)} %bitcast.61, bf16[512,8192]{1,0:T(8,128)(2,1)} %param.16), kind=kOutput, calls=%fused_computation.7 | convolution fusion | flops 2149580800 | bytes 12845056 | tf_op jit(solution)/shard_map/dot_general | solution.py:84
  69.2 70.8 %reduce-scatter.3.cloned.1.call-done = bf16[16,8192]{1,0:T(8,128)(2,1)} async-done(((bf16[256,8192]{1,0:T(8,128)(2,1)}), bf16[16,8192]{1,0:T(8,128)(2,1)}) %reduce-scatter.3.cloned.1.call-update) | async-done | bytes 262160 | tf_op jit(solution)/shard_map/reduce_scatter | solution.py:83
  140.0 1.2 fusion.138
  154.3 38.4 %all-gather.2.cloned.1.call-done = bf16[256,8192]{1,0:T(8,128)(2,1)} async-done(((bf16[16,8192]{1,0:T(8,128)(2,1)}), bf16[256,8192]{1,0:T(8,128)(2,1)}) %all-gather.2.cloned.1.call-update) | async-done | bytes 4194320 | tf_op jit(solution)/shard_map/all_gather | solution.py:92
  192.6 4.4 %fusion.29 = f32[256,128]{0,1:T(8,128)S(1)} fusion(bf16[256,8192]{1,0:T(8,128)(2,1)} %all-gather.2.cloned.1.call-done, f32[8192]{0:T(1024)S(1)} %bitcast.73, bf16[8192,768]{1,0:T(8,128)(2,1)} %param.18), kind=kOutput, calls=%fused_computation.26 | convolution fusion | flops 543162368 | bytes 6455296 | tf_op jit(solution)/shard_map/dot_general | solution.py:100
  197.1 3.2 %fusion.25 = f32[256,128]{0,1:T(8,128)S(1)} fusion(bf16[256,8192]{1,0:T(8,128)(2,1)S(1)} %copy-done.4, f32[8192]{0:T(1024)S(1)} %bitcast.71, bf16[8192,768]{1,0:T(8,128)(2,1)} %param.18), kind=kOutput, calls=%fused_computation.24 | convolution fusion | flops 543162368 | bytes 6455296 | tf_op jit(solution)/shard_map/dot_general | solution.py:100
  200.3 3.2 %fusion.21 = f32[256,128]{0,1:T(8,128)S(1)} fusion(bf16[256,8192]{1,0:T(8,128)(2,1)S(1)} %copy-done.4, f32[8192]{0:T(1024)S(1)} %bitcast.69, bf16[8192,768]{1,0:T(8,128)(2,1)} %param.18), kind=kOutput, calls=%fused_computation.22 | convolution fusion | flops 543162368 | bytes 6455296 | tf_op jit(solution)/shard_map/dot_general | solution.py:100
  203.5 1.5 fusion.17
  205.1 1.5 fusion.13
  206.6 1.5 fusion.9
  208.1 0.9 slice-done.8
  209.0 1.4 fusion.108
  210.4 1.4 fusion.113
  211.8 1.5 fusion.118
  213.3 1.6 fusion.123
  215.5 1.5 fusion.128
  216.9 3.2 %fusion.133 = bf16[256,768]{0,1:T(8,128)(2,1)S(1)} fusion(bf16[256,768]{0,1:T(8,128)(2,1)S(1)} %fusion.128, bf16[8192,768]{1,0:T(8,128)(2,1)} %param.19, bf16[256,8192]{1,0:T(8,128)(2,1)S(1)} %copy-done.5, f32[8192]{0:T(1024)S(1)} %bitcast.64, f32[256,128]{0,1:T(8,128)S(1)} %fusion.9), kind=kOutput, calls=%fused_computation.63 | convolution fusion | flops 543358976 | bytes 6520832 | tf_op jit(solution)/shard_map/dot_general | solution.py:105
  220.2 5.1 %convolution_convert_fusion.1 = bf16[256,8192]{1,0:T(8,128)(2,1)} fusion(bf16[256,768]{0,1:T(8,128)(2,1)S(1)} %fusion.133, bf16[768,8192]{1,0:T(8,128)(2,1)S(1)} %bitcast.59), kind=kOutput, calls=%fused_computation.8 | convolution fusion | flops 3223322624 | bytes 17170432 | tf_op jit(solution)/shard_map/dot_general | solution.py:114
  225.3 71.3 %reduce-scatter.5.cloned.1.call-done = bf16[16,8192]{1,0:T(8,128)(2,1)} async-done(((bf16[256,8192]{1,0:T(8,128)(2,1)}), bf16[16,8192]{1,0:T(8,128)(2,1)}) %reduce-scatter.5.cloned.1.call-update) | async-done | bytes 262160 | tf_op jit(solution)/shard_map/reduce_scatter | solution.py:113
  296.6 1.7 fusion.140
  (49 shorter events, 5.1 us)
Async XLA Ops:
  8.8 51.1 %all-to-all-start = ((bf16[16,16,512]{2,0,1:T(8,128)(2,1)}), bf16[16,16,512]{2,0,1:T(8,128)(2,1)S(1)}, u32[]{:S(2)}, u32[]{:S(2)}) async-start(bf16[16,16,512]{2,0,1:T(8,128)(2,1)} %bitcast.57), calls=%async_computation | async-start | bytes 524288 | tf_op jit(solution)/shard_map/all_to_all | solution.py:61
  16.2 123.8 %reduce-scatter.3.cloned.1.call-start = ((), (), s32[]{:S(2)}) async-start(), calls=%async_computation.3 | async-start | bytes 4456448 | tf_op jit(solution)/shard_map/reduce_scatter | solution.py:83
  69.1 70.9 %copy-start.2 = (bf16[16,8192]{1,0:T(8,128)(2,1)S(1)}, bf16[16,8192]{1,0:T(8,128)(2,1)}, u32[]{:S(2)}) copy-start(bf16[16,8192]{1,0:T(8,128)(2,1)} %param.11) | copy-start | bytes 786436
  69.1 73.2 %copy-start.3 = (s32[96]{0:T(128)S(1)}, s32[96]{0:T(128)}, u32[]{:S(2)}) copy-start(s32[96]{0:T(128)} %param.21) | copy-start | bytes 1156
  69.1 85.0 %copy-start.1 = (f32[2,8192]{1,0:T(2,128)S(1)}, f32[2,8192]{1,0:T(2,128)}, u32[]{:S(2)}) copy-start(f32[2,8192]{1,0:T(2,128)} %param.17) | copy-start | bytes 196612
  69.1 123.5 %all-gather.2.cloned.1.call-start = ((), (), s32[]{:S(2)}) async-start(), calls=%async_computation.4 | async-start | bytes 4456448 | tf_op jit(solution)/shard_map/all_gather | solution.py:92
  141.2 155.4 %copy-start = (bf16[16,8192]{1,0:T(8,128)(2,1)}, bf16[16,8192]{1,0:T(8,128)(2,1)S(1)}, u32[]{:S(2)}) copy-start(bf16[16,8192]{1,0:T(8,128)(2,1)S(1)} %get-tuple-element.3) | copy-start | bytes 786436
  142.1 154.5 %reduce-scatter.5.cloned.1.call-start = ((), (), s32[]{:S(2)}) async-start(), calls=%async_computation.5 | async-start | bytes 4456448 | tf_op jit(solution)/shard_map/reduce_scatter | solution.py:113
  192.6 4.5 %copy-start.4 = (bf16[256,8192]{1,0:T(8,128)(2,1)S(1)}, bf16[256,8192]{1,0:T(8,128)(2,1)}, u32[]{:S(2)}) copy-start(bf16[256,8192]{1,0:T(8,128)(2,1)} %all-gather.2.cloned.1.call-done) | copy-start | bytes 12582916
  192.6 10.8 %slice-start.3 = ((s8[12582912]{0:T(1024)(128)(4,1)}), s8[4194304]{0:T(1024)(128)(4,1)S(1)}, s32[]{:S(2)}) async-start(s8[12582912]{0:T(1024)(128)(4,1)} %bitcast.75), calls=%async_computation.9 | async-start | bytes 8388608
  197.1 6.4 %slice-start.4 = ((s8[12582912]{0:T(1024)(128)(4,1)}), s8[4194304]{0:T(1024)(128)(4,1)S(1)}, s32[]{:S(2)}) async-start(s8[12582912]{0:T(1024)(128)(4,1)} %bitcast.75), calls=%async_computation.10 | async-start | bytes 8388608
  200.3 3.2 %slice-start.5 = ((s8[12582912]{0:T(1024)(128)(4,1)}), s8[4194304]{0:T(1024)(128)(4,1)S(1)}, s32[]{:S(2)}) async-start(s8[12582912]{0:T(1024)(128)(4,1)} %bitcast.75), calls=%async_computation.11 | async-start | bytes 8388608
  203.5 4.6 %slice-start.6 = ((s8[12582912]{0:T(1024)(128)(4,1)}), s8[4194304]{0:T(1024)(128)(4,1)S(1)}, s32[]{:S(2)}) async-start(s8[12582912]{0:T(1024)(128)(4,1)} %bitcast.77), calls=%async_computation.12 | async-start | bytes 8388608
  205.0 3.0 slice-start.7
  206.5 2.4 slice-start.8
  213.3 2.2 copy-start.5
  213.3 6.9 %slice-start = ((s8[12582912]{0:T(1024)(128)(4,1)}), s8[4194304]{0:T(1024)(128)(4,1)S(1)}, s32[]{:S(2)}) async-start(s8[12582912]{0:T(1024)(128)(4,1)} %bitcast.58), calls=%async_computation.6 | async-start | bytes 8388608
  215.5 4.7 %slice-start.1 = ((s8[12582912]{0:T(1024)(128)(4,1)}), s8[4194304]{0:T(1024)(128)(4,1)S(1)}, s32[]{:S(2)}) async-start(s8[12582912]{0:T(1024)(128)(4,1)} %bitcast.58), calls=%async_computation.7 | async-start | bytes 8388608
  216.9 3.3 %slice-start.2 = ((s8[12582912]{0:T(1024)(128)(4,1)}), s8[4194304]{0:T(1024)(128)(4,1)S(1)}, s32[]{:S(2)}) async-start(s8[12582912]{0:T(1024)(128)(4,1)} %bitcast.58), calls=%async_computation.8 | async-start | bytes 8388608
Sparse Core Ops, SparseCore 0:
  69.2 70.7 reduce-scatter.2
  143.0 49.6 all-gather.1
  225.4 71.1 reduce-scatter.4
where the time goes:
time: 305 us
  waiting for transfers between devices  181 us (59%)
  blocking collectives  42.6 us (14%)
  matrix products  40 us (13%)
  between operations  25.2 us (8%)
  starting transfers between devices  7.69 us (3%)
  other arithmetic  4.74 us (2%)
  local copies, waits for them, and re-layouts  4.1 us (1%)
    reduce_scatter x1, waiting for transfers between devices, local(): lax.psum_scatter(jnp.dot(picked, down_weight, preferred_element_type=jnp....  71.3 us
    reduce_scatter x1, waiting for transfers between devices, local(): lax.psum_scatter(jnp.dot(picked, out_weight, preferred_element_type=jnp.f...  70.8 us
    all_gather x1, waiting for transfers between devices, local(): row_piece = lax.all_gather(sent_rows, 'mp', axis=0, tiled=True)  38.4 us
    all_gather x1, blocking collectives, local(): lax.all_gather(key_proj, 'mp', axis=0, tiled=True)  23.5 us
    all_gather x1, blocking collectives, local(): lax.all_gather(values, 'mp', axis=0, tiled=True)  19.1 us
    dot_general x6, matrix products, local(): jnp.dot(slice_input, gate_weight[:, slice_pos * SLICE:(slice_pos + 1) * S...  15.3 us
    dot_general x6, matrix products, local(): jnp.dot(slice_input, up_weight[:, slice_pos * SLICE:(slice_pos + 1) * SLI...  10.6 us
    dot_general x1, matrix products, local(): jnp.dot(picked, out_weight, preferred_element_type=jnp.float32)  7.71 us
  transfers between devices with their start and end apart: 4, of which 3 were waited for; matrix products, arithmetic and copies ran while one was open for 1% of the time, Pallas kernels for 0%

commit v1 on v0

v1 whole, which is shorter than its diff:
```python
import functools
import math

import jax
import jax.numpy as jnp
import numpy as np
from jax import lax
from jax.experimental import pallas as pl
from jax.experimental.pallas import tpu as pltpu
from jax.sharding import PartitionSpec as P

QUERY_HEADS = 64
HEAD_SIZE = 128
SLICE = 128
CHUNKS = 8
MESH = pl.DeviceIdType.MESH
F32 = jnp.float32
BF16 = jnp.bfloat16


def place(zs):
    me = lax.axis_index("mp")
    core = lax.rem(me, 2)
    y = lax.rem(me // 2, 2)
    z = me // 4

    def dev(z_, y_, core_):
        return {"mp": (z_ * 2 + y_) * 2 + core_}

    return core, y, z, dev


def project_kernel(zs, gather, *refs):
    if gather:
        (a_ref, w_hbm, res_ref, out_ref, all_hbm, w, part, from_core, pair, from_y, quad, from_z,
         w_sem, cs, cr, ys, yr, zsend, zrecv, whole, gzs, gzr, gys, gyr, gcs, gcr, out_sem) = refs
    else:
        (a_ref, w_hbm, res_ref, out_ref, w, part, from_core, pair, from_y, quad, from_z,
         w_sem, cs, cr, ys, yr, zsend, zrecv) = refs
    core, y, z, dev = place(zs)
    n, half, cw = from_core.shape
    tok = half // 2 // zs

    def w_copy(j):
        cols = pl.ds(pl.multiple_of(j * cw, cw), cw)
        return pltpu.make_async_copy(w_hbm.at[:, cols], w.at[j], w_sem.at[j])

    def remote(src, dst, s, r, to):
        return pltpu.make_async_remote_copy(
            src_ref=src, dst_ref=dst, send_sem=s, recv_sem=r, device_id=to, device_id_type=MESH
        )

    def core_copy(j):
        return remote(part.at[j, 1 - core], from_core.at[j], cs.at[j], cr.at[j], dev(z, y, 1 - core))

    def y_copy(j):
        return remote(pair.at[j, 1 - y], from_y.at[j], ys.at[j], yr.at[j], dev(z, 1 - y, core))

    def z_copy(j, d):
        to = lax.rem(z + d, zs)
        return remote(
            quad.at[j, to], from_z.at[j, d], zsend.at[j, d], zrecv.at[j, d], dev(to, y, core)
        )

    def gz_copy(j, d):
        to = lax.rem(z + d, zs)
        mine = whole.at[j, core, y, z]
        return remote(mine, mine, gzs.at[j, d], gzr.at[j, d], dev(to, y, core))

    def gy_copy(j):
        mine = whole.at[j, core, y]
        return remote(mine, mine, gys.at[j], gyr.at[j], dev(z, 1 - y, core))

    def gc_copy(j):
        mine = whole.at[j, core]
        return remote(mine, mine, gcs.at[j], gcr.at[j], dev(z, y, 1 - core))

    def out_copy(j):
        return pltpu.make_async_copy(whole.at[j], all_hbm.at[j], out_sem.at[j])

    @pl.loop(0, n)
    def _(j):
        w_copy(j).start()

    barrier = pltpu.get_barrier_semaphore()
    partners = [dev(z, y, 1 - core), dev(z, 1 - y, core)]
    partners += [dev(lax.rem(z + d, zs), y, core) for d in range(1, zs)]
    for to in partners:
        pl.semaphore_signal(barrier, inc=1, device_id=to, device_id_type=MESH)
    pl.semaphore_wait(barrier, len(partners))

    def multiply(j):
        w_copy(j).wait()
        res = jnp.dot(a_ref[...], w[j], preferred_element_type=F32).astype(BF16)
        part[j, 0] = res[:half]
        part[j, 1] = res[half:]
        core_copy(j).start()

    def add_core(j):
        core_copy(j).wait_recv()
        res = (part[j, core].astype(F32) + from_core[j].astype(F32)).astype(BF16)
        pair[j, 0] = res[: half // 2]
        pair[j, 1] = res[half // 2 :]
        y_copy(j).start()

    def add_y(j):
        y_copy(j).wait_recv()
        res = (pair[j, y].astype(F32) + from_y[j].astype(F32)).astype(BF16)
        quad[j] = res.reshape(zs, tok, cw)
        for d in range(1, zs):
            z_copy(j, d).start()

    def add_z(j):
        total = quad[j, z].astype(F32)
        for d in range(1, zs):
            z_copy(j, d).wait_recv()
            total += from_z[j, d].astype(F32)
        cols = pl.ds(pl.multiple_of(j * cw, cw), cw)
        res = (res_ref[:, cols].astype(F32) + total).astype(BF16)
        out_ref[:, cols] = res
        if gather:
            whole[j, core, y, z] = res
            for d in range(1, zs):
                gz_copy(j, d).start()

    def spread_y(j):
        for d in range(1, zs):
            gz_copy(j, d).wait_recv()
        gy_copy(j).start()

    def spread_core(j):
        gy_copy(j).wait_recv()
        gc_copy(j).start()

    def finish(j):
        gc_copy(j).wait_recv()
        out_copy(j).start()

    stages = [(0, multiply), (1, add_core), (2, add_y), (4, add_z)]
    if gather:
        stages += [(6, spread_y), (8, spread_core), (9, finish)]

    @pl.loop(0, n + stages[-1][0])
    def _(i):
        for lag, stage in stages:
            @pl.when((i >= lag) & (i < n + lag))
            def _(stage=stage, lag=lag):
                stage(i - lag)

    @pl.loop(0, n)
    def _(j):
        core_copy(j).wait_send()
        y_copy(j).wait_send()
        for d in range(1, zs):
            z_copy(j, d).wait_send()
        if gather:
            for d in range(1, zs):
                gz_copy(j, d).wait_send()
            gy_copy(j).wait_send()
            gc_copy(j).wait_send()
            out_copy(j).wait()


def project(a, weight, residual, zs, gather):
    rows, depth = a.shape
    width = weight.shape[1]
    tok = residual.shape[0]
    n, cw, half = CHUNKS, width // CHUNKS, rows // 2
    dma = pltpu.SemaphoreType.DMA
    vmem = pl.BlockSpec(memory_space=pltpu.VMEM)
    scratch = [
        pltpu.VMEM((n, depth, cw), BF16),
        pltpu.VMEM((n, 2, half, cw), BF16),
        pltpu.VMEM((n, half, cw), BF16),
        pltpu.VMEM((n, 2, half // 2, cw), BF16),
        pltpu.VMEM((n, half // 2, cw), BF16),
        pltpu.VMEM((n, zs, tok, cw), BF16),
        pltpu.VMEM((n, zs, tok, cw), BF16),
        dma((n,)), dma((n,)), dma((n,)), dma((n,)), dma((n,)), dma((n, zs)), dma((n, zs)),
    ]
    outs = [jax.ShapeDtypeStruct((tok, width), BF16)]
    out_specs = [vmem]
    if gather:
        outs.append(jax.ShapeDtypeStruct((n, 2, 2, zs, tok, cw), BF16))
        out_specs.append(pl.BlockSpec(memory_space=pl.ANY))
        scratch += [
            pltpu.VMEM((n, 2, 2, zs, tok, cw), BF16),
            dma((n, zs)), dma((n, zs)), dma((n,)), dma((n,)), dma((n,)), dma((n,)), dma((n,)),
        ]
    res = pl.pallas_call(
        functools.partial(project_kernel, zs, gather),
        out_shape=outs,
        in_specs=[vmem, pl.BlockSpec(memory_space=pl.ANY), vmem],
        out_specs=out_specs,
        scratch_shapes=scratch,
        compiler_params=pltpu.CompilerParams(
            collective_id=0 if gather else 1, has_side_effects=True, vmem_limit_bytes=56 << 20
        ),
        name="attn_out" if gather else "ffn_down",
    )(a, weight, residual)
    return res


def ffn_kernel(which, x_ref, gain_ref, gate_ref, up_ref, hid_ref, inputs):
    n, rows, cw = x_ref.shape
    s = pl.program_id(0)

    @pl.when(s == 0)
    def _():
        block = 64

        @pl.loop(0, rows // block)
        def _(b):
            at = pl.ds(pl.multiple_of(b * block, block), block)
            square = jnp.zeros((block, 1), F32)
            for j in range(n):
                x = x_ref[j, at, :].astype(F32)
                square += jnp.sum(x * x, axis=1, keepdims=True)
            inv = lax.rsqrt(square / (n * cw) + 1e-05)
            for j in range(n):
                x = (x_ref[j, at, :].astype(F32) * inv).astype(BF16).astype(F32)
                for f in range(gain_ref.shape[0]):
                    g = gain_ref[f : f + 1, j * cw : (j + 1) * cw]
                    inputs[f, j, at, :] = (x * g).astype(BF16)

    f = which[s]
    acc = jnp.zeros((rows, 2 * SLICE), F32)
    for j in range(n):
        k = slice(j * cw, (j + 1) * cw)
        both = jnp.concatenate([gate_ref[k, :], up_ref[k, :]], axis=1)
        acc += jnp.dot(inputs[f, j], both, preferred_element_type=F32)
    gate, up = acc[:, :SLICE], acc[:, SLICE:]
    hid_ref[...] = (gate / (1.0 + jnp.exp(-gate)) * up).astype(BF16)


def ffn_hidden(which, x, gain, gate_weight, up_weight):
    n, rows, cw = x.shape
    width, units = gate_weight.shape
    return pl.pallas_call(
        ffn_kernel,
        out_shape=jax.ShapeDtypeStruct((rows, units), BF16),
        grid_spec=pltpu.PrefetchScalarGridSpec(
            num_scalar_prefetch=1,
            grid=(units // SLICE,),
            in_specs=[
                pl.BlockSpec((n, rows, cw), lambda s, w: (0, 0, 0), pipeline_mode=pl.Buffered(1)),
                pl.BlockSpec(gain.shape, lambda s, w: (0, 0), pipeline_mode=pl.Buffered(1)),
                pl.BlockSpec((width, SLICE), lambda s, w: (0, s)),
                pl.BlockSpec((width, SLICE), lambda s, w: (0, s)),
            ],
            out_specs=pl.BlockSpec((rows, SLICE), lambda s, w: (0, s)),
            scratch_shapes=[pltpu.VMEM((gain.shape[0], n, rows, cw), BF16)],
        ),
        compiler_params=pltpu.CompilerParams(vmem_limit_bytes=56 << 20),
        name="ffn_hidden",
    )(which, x, gain, gate_weight, up_weight)


def attention(query_rows, key_cols, value_cols, query_pos, seq_lens, local_heads):
    count = query_rows.shape[0]
    seq_ends = jnp.cumsum(seq_lens)
    key_pos = jnp.arange(count, dtype=jnp.int32)

    def segment_of(positions):
        return jnp.sum((positions[:, None] >= seq_ends[None, :]).astype(jnp.int32), axis=1)

    visible = (segment_of(query_pos)[:, None] == segment_of(key_pos)[None, :]) & (
        key_pos[None, :] <= query_pos[:, None]
    )
    scores = jnp.einsum(
        "thd,sd->hts",
        query_rows.reshape(count, local_heads, HEAD_SIZE),
        key_cols,
        preferred_element_type=F32,
    ) * (1.0 / math.sqrt(HEAD_SIZE))
    masked = jnp.where(visible[None], scores, -1e30)
    highest = jnp.max(masked, axis=-1, keepdims=True)
    expo = jnp.where(visible[None], jnp.exp(masked - highest), 0.0)
    probs = (expo / jnp.sum(expo, axis=-1, keepdims=True)).astype(BF16)
    return (
        jnp.einsum("hts,sd->thd", probs, value_cols, preferred_element_type=F32)
        .astype(BF16)
        .reshape(count, local_heads * HEAD_SIZE)
    )


def local(tokens, queries, key_proj, values, seq_lens, out_weight, ffn_gain, gate_weight, up_weight,
          down_weight, slice_table):
    tok = tokens.shape[0]
    mp = lax.axis_size("mp")
    zs = mp // 4
    count = tok * mp
    me = lax.axis_index("mp")
    heads_kv = key_proj.shape[1] // HEAD_SIZE
    per_group = QUERY_HEADS // heads_kv
    local_heads = QUERY_HEADS // mp

    kv_heads = np.arange(mp) * local_heads // per_group
    repeat = mp // heads_kv
    assert (kv_heads == np.arange(mp) // repeat).all()

    def for_devices(rows):
        return jnp.repeat(rows.reshape(tok, heads_kv, 1, HEAD_SIZE), repeat, axis=2).reshape(
            tok, mp, HEAD_SIZE
        )

    sent = jnp.concatenate(
        [queries.reshape(tok, mp, -1), for_devices(key_proj), for_devices(values)], axis=2
    )
    got = lax.all_to_all(sent.transpose(1, 0, 2), "mp", split_axis=0, concat_axis=0, tiled=True)
    q_width = local_heads * HEAD_SIZE
    key_cols = got[:, :, q_width : q_width + HEAD_SIZE].reshape(count, HEAD_SIZE)
    value_cols = got[:, :, q_width + HEAD_SIZE :].reshape(count, HEAD_SIZE)

    def reorder(rows):
        return rows.reshape(zs, 2, 2, tok, -1).transpose(2, 1, 0, 3, 4)

    query_rows = reorder(got[:, :, :q_width]).reshape(count, q_width)
    query_pos = reorder(jnp.arange(count, dtype=jnp.int32)).reshape(count)
    context = attention(query_rows, key_cols, value_cols, query_pos, seq_lens, local_heads)
    stream, gathered = project(context, out_weight, tokens, zs, True)
    slices = gate_weight.shape[1] // SLICE
    which = lax.dynamic_slice_in_dim(slice_table, me * slices, slices)
    x = gathered.reshape(CHUNKS, count, -1)
    hidden = ffn_hidden(which, x, ffn_gain, gate_weight, up_weight)
    (mixed,) = project(hidden, down_weight, stream, zs, False)
    return (stream, mixed)


def solution(mesh):
    placed = (
        P(("groups", "mp"), None),
        P(("groups", "mp"), None),
        P(("groups", "mp"), None),
        P(("groups", "mp"), None),
        P("groups"),
        P("mp", None),
        P(),
        P(None, "mp"),
        P(None, "mp"),
        P("mp", None),
        P(),
    )
    return jax.shard_map(
        local,
        mesh=mesh,
        in_specs=placed,
        out_specs=(P(("groups", "mp"), None), P(("groups", "mp"), None)),
        check_vma=False,
    )
```

time: 305 us -> 149 us (0.49)
  waiting for transfers between devices: 181 us -> 9.83 us
  Pallas kernels: 0 us -> 120 us
  blocking collectives: 42.6 us -> 0 us
  matrix products: 40 us -> 1.37 us
  between operations: 25.2 us -> 0.74 us
  local copies, waits for them, and re-layouts: 4.1 us -> 8.17 us
  other arithmetic: 4.74 us -> 1.06 us
    reduce_scatter x2 -> x0, waiting for transfers between devices: 142 us -> none  [the longest x1 71.3 us: local(): lax.psum_scatter(jnp.dot(picked, down_weight, preferred_element_type=jnp....]
    pallas_call x0 -> x3, Pallas kernels: none -> 120 us  [the longest x2 102 us: project(): pl.pallas_call(functools.partial(project_kernel, zs, gather), out_shape=o...]
    all_gather x2 -> x0, blocking collectives: 42.6 us -> none  [the longest x1 23.5 us: local(): lax.all_gather(key_proj, 'mp', axis=0, tiled=True)]
    dot_general x15 -> x1, matrix products: 39.4 us -> 0.79 us  [attention(): jnp.einsum('hts,sd->thd', probs, value_cols, preferred_element_type=F32)]
    all_gather x1 -> x0, waiting for transfers between devices: 38.4 us -> none  [local(): row_piece = lax.all_gather(sent_rows, 'mp', axis=0, tiled=True)]
    all_to_all x1, waiting for transfers between devices: 0.01 us -> 9.83 us  [local(): lax.all_to_all(sent.transpose(1, 0, 2), 'mp', split_axis=0, concat_axis=0...]
    unnamed x30 -> x7, local copies, waits for them, and re-layouts: 1.48 us -> 4.94 us
  transfers between devices with their start and end apart: 4 -> 1, of which waited for: 3 -> 1; matrix products, arithmetic and copies ran while one was open for 1% -> 2% of each run, Pallas kernels for 0% -> 0%
where the time goes in v1:
time: 149 us
  Pallas kernels  120 us (81%)
  waiting for transfers between devices  9.83 us (7%)
  local copies, waits for them, and re-layouts  8.17 us (5%)
  starting transfers between devices  7.39 us (5%)
    pallas_call x2, Pallas kernels, project(): pl.pallas_call(functools.partial(project_kernel, zs, gather), out_shape=o...  102 us
    pallas_call x1, Pallas kernels, ffn_hidden(): pl.pallas_call(ffn_kernel, out_shape=jax.ShapeDtypeStruct((rows, units),...  17.8 us
    all_to_all x1, waiting for transfers between devices, local(): lax.all_to_all(sent.transpose(1, 0, 2), 'mp', split_axis=0, concat_axis=0...  9.83 us
    all_to_all x1, starting transfers between devices, local(): lax.all_to_all(sent.transpose(1, 0, 2), 'mp', split_axis=0, concat_axis=0...  7.39 us
    unnamed x7, local copies, waits for them, and re-layouts  4.94 us
  transfers between devices with their start and end apart: 1, of which 1 were waited for; matrix products, arithmetic and copies ran while one was open for 2% of the time, Pallas kernels for 0%

profile of v1, /device:TPU:0, one launch (start us, length us, event | category | flops | bytes accessed | tf_op | source)
XLA Modules:
  0.0 148.6 jit_solution(4702855495160731690)
XLA Ops:
  0.6 0.8 copy.50
  1.4 0.8 copy.51
  2.2 1.0 copy.49
  3.3 0.9 copy.39
  4.2 7.4 %all-to-all-start = ((bf16[16,16,768]{2,1,0:T(8,128)(2,1)}), bf16[16,16,768]{2,1,0:T(8,128)(2,1)S(1)}, u32[]{:S(2)}, u32[]{:S(2)}) async-start(bf16[16,16,768]{2,1,0:T(8,128)(2,1)} %copy.39), calls=%async_computation | async-start | bytes 786432 | tf_op jit(solution)/shard_map/all_to_all | solution.py:310
  11.6 0.8 reduce-window.8
  12.4 0.1 ge.12
  12.5 1.2 dynamic_slice.3.which
  13.7 0.1 convert_reduce_fusion
  13.8 0.1 fusion.7
  13.9 9.8 %all-to-all-done = bf16[16,16,768]{2,1,0:T(8,128)(2,1)S(1)} async-done(((bf16[16,16,768]{2,1,0:T(8,128)(2,1)}), bf16[16,16,768]{2,1,0:T(8,128)(2,1)S(1)}, u32[]{:S(2)}, u32[]{:S(2)}) %all-to-all-start) | async-done | bytes 393248 | tf_op jit(solution)/shard_map/all_to_all | solution.py:310
  23.8 0.1 reshape_reshape.11
  23.9 0.6 fusion.26
  24.5 0.8 convolution_convert_fusion
  25.3 0.8 copy.48.refs_0_
  26.2 65.0 %attn_out.1 = (bf16[16,8192]{1,0:T(8,128)(2,1)}, bf16[8,2,2,4,16,1024]{5,4,3,2,1,0:T(8,128)(2,1)}) custom-call(bf16[256,512]{1,0:T(8,128)(2,1)} %copy.48.refs_0_, bf16[512,8192]{1,0:T(8,128)(2,1)} %refs_1_.2, bf16[16,8192]{1,0:T(8,128)(2,1)} %refs_2_.1), custom_call_target="tpu_custom_call" | custom-call | tf_op jit(solution)/shard_map/attn_out/pallas_call | solution.py:190
  91.1 17.8 %ffn_hidden.1.refs_0_ = bf16[256,768]{1,0:T(8,128)(2,1)} custom-call(s32[6]{0:T(128)} %dynamic_slice.3.which, bf16[8,256,1024]{2,1,0:T(8,128)(2,1)} %bitcast.49, f32[2,8192]{1,0:T(2,128)} %gain_ref.1, bf16[8192,768]{1,0:T(8,128)(2,1)} %gate_ref.1, bf16[8192,768]{1,0:T(8,128)(2,1)} %up_ref.1), custom_call_target="tpu_custom_call" | custom-call | tf_op jit(solution)/shard_map/ffn_hidden/pallas_call | solution.py:239
  109.0 0.0 copy-start
  109.0 37.2 %ffn_down.1 = bf16[16,8192]{1,0:T(8,128)(2,1)} custom-call(bf16[256,768]{1,0:T(8,128)(2,1)} %ffn_hidden.1.refs_0_, bf16[768,8192]{1,0:T(8,128)(2,1)} %refs_1_.3, bf16[16,8192]{1,0:T(8,128)(2,1)} %get-tuple-element.12.refs_2_), custom_call_target="tpu_custom_call" | custom-call | tf_op jit(solution)/shard_map/ffn_down/pallas_call | solution.py:190
  146.2 0.0 copy-done
  146.2 0.7 copy.68
  146.9 1.7 %copy.69 = bf16[16,8192]{1,0:T(8,128)(2,1)} copy(bf16[16,8192]{1,0:T(8,128)(2,1)} %ffn_down.1) | data formatting | bytes 524288
  (7 shorter events, 0.2 us)
Async XLA Ops:
  4.2 19.6 %all-to-all-start = ((bf16[16,16,768]{2,1,0:T(8,128)(2,1)}), bf16[16,16,768]{2,1,0:T(8,128)(2,1)S(1)}, u32[]{:S(2)}, u32[]{:S(2)}) async-start(bf16[16,16,768]{2,1,0:T(8,128)(2,1)} %copy.39), calls=%async_computation | async-start | bytes 786432 | tf_op jit(solution)/shard_map/all_to_all | solution.py:310
  109.0 37.3 %copy-start = (bf16[16,8192]{1,0:T(8,128)(2,1)S(1)}, bf16[16,8192]{1,0:T(8,128)(2,1)}, u32[]{:S(2)}) copy-start(bf16[16,8192]{1,0:T(8,128)(2,1)} %get-tuple-element.12.refs_2_) | copy-start | bytes 786436

commit v2 on v1

v2 whole, which is shorter than its diff:
```python
import functools
import math

import jax
import jax.numpy as jnp
import numpy as np
from jax import lax
from jax.experimental import pallas as pl
from jax.experimental.pallas import tpu as pltpu
from jax.sharding import PartitionSpec as P

QUERY_HEADS = 64
HEAD_SIZE = 128
SLICE = 128
CHUNKS = 8
MESH = pl.DeviceIdType.MESH
F32 = jnp.float32
BF16 = jnp.bfloat16


def place(zs):
    me = lax.axis_index("mp")
    core = lax.rem(me, 2)
    y = lax.rem(me // 2, 2)
    z = me // 4

    def dev(z_, y_, core_):
        return {"mp": (z_ * 2 + y_) * 2 + core_}

    return core, y, z, dev


def layer_kernel(zs, slices, *refs):
    (which, a_ref, res_ref, gain_ref, w_hbm, gate_hbm, up_hbm, down_hbm, stream_ref, mixed_ref,
     w, gate, up, part, from_core, pair, from_y, quad, from_z, whole, gained, square, acc, hidden,
     w_sem, gate_sem, up_sem, cs, cr, ys, yr, zsend, zrecv, gzs, gzr, gys, gyr, gcs, gcr) = refs
    core, y, z, dev = place(zs)
    n, half, cw = from_core.shape
    rows = 2 * half
    tok = half // 2 // zs

    def columns(j):
        return pl.ds(pl.multiple_of(j * cw, cw), cw)

    def w_copy(j, first):
        src = w_hbm if first else down_hbm
        dst = w.at[j, pl.ds(0, src.shape[0])]
        return pltpu.make_async_copy(src.at[:, columns(j)], dst, w_sem.at[j])

    def gate_copy(j):
        return pltpu.make_async_copy(gate_hbm.at[columns(j), :], gate.at[j], gate_sem.at[j])

    def up_copy(j):
        return pltpu.make_async_copy(up_hbm.at[columns(j), :], up.at[j], up_sem.at[j])

    def remote(src, dst, s, r, to):
        return pltpu.make_async_remote_copy(
            src_ref=src, dst_ref=dst, send_sem=s, recv_sem=r, device_id=to, device_id_type=MESH
        )

    def core_copy(j):
        return remote(part.at[j, 1 - core], from_core.at[j], cs.at[j], cr.at[j], dev(z, y, 1 - core))

    def y_copy(j):
        return remote(pair.at[j, 1 - y], from_y.at[j], ys.at[j], yr.at[j], dev(z, 1 - y, core))

    def z_copy(j, d):
        to = lax.rem(z + d, zs)
        return remote(
            quad.at[j, to], from_z.at[j, d], zsend.at[j, d], zrecv.at[j, d], dev(to, y, core)
        )

    def gz_copy(j, d):
        to = lax.rem(z + d, zs)
        mine = whole.at[j, core, y, z]
        return remote(mine, mine, gzs.at[j, d], gzr.at[j, d], dev(to, y, core))

    def gy_copy(j):
        mine = whole.at[j, core, y]
        return remote(mine, mine, gys.at[j], gyr.at[j], dev(z, 1 - y, core))

    def gc_copy(j):
        mine = whole.at[j, core]
        return remote(mine, mine, gcs.at[j], gcr.at[j], dev(z, y, 1 - core))

    @pl.loop(0, n)
    def _(j):
        w_copy(j, True).start()

    barrier = pltpu.get_barrier_semaphore()
    partners = [dev(z, y, 1 - core), dev(z, 1 - y, core)]
    partners += [dev(lax.rem(z + d, zs), y, core) for d in range(1, zs)]
    for to in partners:
        pl.semaphore_signal(barrier, inc=1, device_id=to, device_id_type=MESH)
    pl.semaphore_wait(barrier, len(partners))

    @pl.loop(0, n)
    def _(j):
        gate_copy(j).start()
        up_copy(j).start()

    square[...] = jnp.zeros_like(square)
    acc[...] = jnp.zeros_like(acc)

    def multiply(j, first):
        lhs = a_ref if first else hidden
        w_copy(j, first).wait()
        res = jnp.dot(
            lhs[...], w[j, : lhs.shape[1], :], preferred_element_type=F32
        ).astype(BF16)
        part[j, 0] = res[:half]
        part[j, 1] = res[half:]
        core_copy(j).start()
        if first:
            w_copy(j, False).start()

    def add_core(j):
        core_copy(j).wait_recv()
        res = (part[j, core].astype(F32) + from_core[j].astype(F32)).astype(BF16)
        pair[j, 0] = res[: half // 2]
        pair[j, 1] = res[half // 2 :]
        y_copy(j).start()

    def add_y(j):
        y_copy(j).wait_recv()
        res = (pair[j, y].astype(F32) + from_y[j].astype(F32)).astype(BF16)
        quad[j] = res.reshape(zs, tok, cw)
        for d in range(1, zs):
            z_copy(j, d).start()

    def add_z(j, first):
        total = quad[j, z].astype(F32)
        for d in range(1, zs):
            z_copy(j, d).wait_recv()
            total += from_z[j, d].astype(F32)
        before = res_ref if first else stream_ref
        res = (before[:, columns(j)].astype(F32) + total).astype(BF16)
        if first:
            stream_ref[:, columns(j)] = res
            whole[j, core, y, z] = res
            for d in range(1, zs):
                gz_copy(j, d).start()
        else:
            mixed_ref[:, columns(j)] = res

    def spread_y(j):
        for d in range(1, zs):
            gz_copy(j, d).wait_recv()
        gy_copy(j).start()

    def spread_core(j):
        gy_copy(j).wait_recv()
        gc_copy(j).start()

    def consume(j):
        gc_copy(j).wait_recv()
        gate_copy(j).wait()
        up_copy(j).wait()
        for c in range(2):
            for q in range(2):
                x = whole[j, c, q].reshape(zs * tok, cw).astype(F32)
                at = slice((c * 2 + q) * zs * tok, (c * 2 + q + 1) * zs * tok)
                total = square[at, :]
                for k in range(0, cw, 128):
                    total += x[:, k : k + 128] * x[:, k : k + 128]
                square[at, :] = total
                for f in range(gained.shape[0]):
                    gained[f, at, :] = (x * gain_ref[f : f + 1, columns(j)]).astype(BF16)
        for s in range(slices):
            cols = slice(s * SLICE, (s + 1) * SLICE)
            both = jnp.concatenate([gate[j, :, cols], up[j, :, cols]], axis=1)
            acc[s] += jnp.dot(gained[which[s]], both, preferred_element_type=F32)

    def send_waits(j):
        core_copy(j).wait_send()
        y_copy(j).wait_send()
        for d in range(1, zs):
            z_copy(j, d).wait_send()

    def run(stages):
        @pl.loop(0, n + stages[-1][0])
        def _(i):
            for lag, stage in stages:
                @pl.when((i >= lag) & (i < n + lag))
                def _(stage=stage, lag=lag):
                    stage(i - lag)

    run([
        (0, functools.partial(multiply, first=True)), (1, add_core), (2, add_y),
        (4, functools.partial(add_z, first=True)), (6, spread_y), (8, spread_core), (9, consume),
    ])

    inv = lax.rsqrt(jnp.sum(square[...], axis=1, keepdims=True) / (n * cw) + 1e-05)
    for s in range(slices):
        both = acc[s] * inv
        g, u = both[:, :SLICE], both[:, SLICE:]
        hidden[:, s * SLICE : (s + 1) * SLICE] = (g / (1.0 + jnp.exp(-g)) * u).astype(BF16)

    @pl.loop(0, n)
    def _(j):
        send_waits(j)
        for d in range(1, zs):
            gz_copy(j, d).wait_send()
        gy_copy(j).wait_send()
        gc_copy(j).wait_send()

    run([
        (0, functools.partial(multiply, first=False)), (1, add_core), (2, add_y),
        (4, functools.partial(add_z, first=False)),
    ])

    @pl.loop(0, n)
    def _(j):
        send_waits(j)


def layer(which, context, tokens, gain, out_weight, gate_weight, up_weight, down_weight, zs):
    rows, depth = context.shape
    tok, width = tokens.shape
    units = down_weight.shape[0]
    slices = units // SLICE
    n, cw, half = CHUNKS, width // CHUNKS, rows // 2
    dma = pltpu.SemaphoreType.DMA
    vmem = pl.BlockSpec(memory_space=pltpu.VMEM)
    hbm = pl.BlockSpec(memory_space=pl.ANY)
    return pl.pallas_call(
        functools.partial(layer_kernel, zs, slices),
        out_shape=[jax.ShapeDtypeStruct((tok, width), BF16)] * 2,
        in_specs=[pl.BlockSpec(memory_space=pltpu.SMEM)] + [vmem] * 3 + [hbm] * 4,
        out_specs=[vmem] * 2,
        scratch_shapes=[
            pltpu.VMEM((n, max(depth, units), cw), BF16),
            pltpu.VMEM((n, cw, units), BF16),
            pltpu.VMEM((n, cw, units), BF16),
            pltpu.VMEM((n, 2, half, cw), BF16),
            pltpu.VMEM((n, half, cw), BF16),
            pltpu.VMEM((n, 2, half // 2, cw), BF16),
            pltpu.VMEM((n, half // 2, cw), BF16),
            pltpu.VMEM((n, zs, tok, cw), BF16),
            pltpu.VMEM((n, zs, tok, cw), BF16),
            pltpu.VMEM((n, 2, 2, zs, tok, cw), BF16),
            pltpu.VMEM((gain.shape[0], rows, cw), BF16),
            pltpu.VMEM((rows, 128), F32),
            pltpu.VMEM((slices, rows, 2 * SLICE), F32),
            pltpu.VMEM((rows, units), BF16),
            dma((n,)), dma((n,)), dma((n,)),
            dma((n,)), dma((n,)), dma((n,)), dma((n,)), dma((n, zs)), dma((n, zs)),
            dma((n, zs)), dma((n, zs)), dma((n,)), dma((n,)), dma((n,)), dma((n,)),
        ],
        compiler_params=pltpu.CompilerParams(
            collective_id=0, has_side_effects=True, vmem_limit_bytes=60 << 20
        ),
        name="layer",
    )(which, context, tokens, gain, out_weight, gate_weight, up_weight, down_weight)


def attention(query_rows, key_cols, value_cols, query_pos, seq_lens, local_heads):
    count = query_rows.shape[0]
    seq_ends = jnp.cumsum(seq_lens)
    key_pos = jnp.arange(count, dtype=jnp.int32)

    def segment_of(positions):
        return jnp.sum((positions[:, None] >= seq_ends[None, :]).astype(jnp.int32), axis=1)

    visible = (segment_of(query_pos)[:, None] == segment_of(key_pos)[None, :]) & (
        key_pos[None, :] <= query_pos[:, None]
    )
    scores = jnp.einsum(
        "thd,sd->hts",
        query_rows.reshape(count, local_heads, HEAD_SIZE),
        key_cols,
        preferred_element_type=F32,
    ) * (1.0 / math.sqrt(HEAD_SIZE))
    masked = jnp.where(visible[None], scores, -1e30)
    highest = jnp.max(masked, axis=-1, keepdims=True)
    expo = jnp.where(visible[None], jnp.exp(masked - highest), 0.0)
    probs = (expo / jnp.sum(expo, axis=-1, keepdims=True)).astype(BF16)
    return (
        jnp.einsum("hts,sd->thd", probs, value_cols, preferred_element_type=F32)
        .astype(BF16)
        .reshape(count, local_heads * HEAD_SIZE)
    )


def local(tokens, queries, key_proj, values, seq_lens, out_weight, ffn_gain, gate_weight, up_weight,
          down_weight, slice_table):
    tok = tokens.shape[0]
    mp = lax.axis_size("mp")
    zs = mp // 4
    count = tok * mp
    me = lax.axis_index("mp")
    heads_kv = key_proj.shape[1] // HEAD_SIZE
    per_group = QUERY_HEADS // heads_kv
    local_heads = QUERY_HEADS // mp

    kv_heads = np.arange(mp) * local_heads // per_group
    repeat = mp // heads_kv
    assert (kv_heads == np.arange(mp) // repeat).all()

    def for_devices(rows):
        return jnp.repeat(rows.reshape(tok, heads_kv, 1, HEAD_SIZE), repeat, axis=2).reshape(
            tok, mp, HEAD_SIZE
        )

    sent = jnp.concatenate(
        [queries.reshape(tok, mp, -1), for_devices(key_proj), for_devices(values)], axis=2
    )
    got = lax.all_to_all(sent.transpose(1, 0, 2), "mp", split_axis=0, concat_axis=0, tiled=True)
    q_width = local_heads * HEAD_SIZE
    key_cols = got[:, :, q_width : q_width + HEAD_SIZE].reshape(count, HEAD_SIZE)
    value_cols = got[:, :, q_width + HEAD_SIZE :].reshape(count, HEAD_SIZE)

    def reorder(rows):
        return rows.reshape(zs, 2, 2, tok, -1).transpose(2, 1, 0, 3, 4)

    query_rows = reorder(got[:, :, :q_width]).reshape(count, q_width)
    query_pos = reorder(jnp.arange(count, dtype=jnp.int32)).reshape(count)
    context = attention(query_rows, key_cols, value_cols, query_pos, seq_lens, local_heads)
    slices = gate_weight.shape[1] // SLICE
    which = lax.dynamic_slice_in_dim(slice_table, me * slices, slices)
    stream, mixed = layer(
        which, context, tokens, ffn_gain, out_weight, gate_weight, up_weight, down_weight, zs
    )
    return (stream, mixed)


def solution(mesh):
    placed = (
        P(("groups", "mp"), None),
        P(("groups", "mp"), None),
        P(("groups", "mp"), None),
        P(("groups", "mp"), None),
        P("groups"),
        P("mp", None),
        P(),
        P(None, "mp"),
        P(None, "mp"),
        P("mp", None),
        P(),
    )
    return jax.shard_map(
        local,
        mesh=mesh,
        in_specs=placed,
        out_specs=(P(("groups", "mp"), None), P(("groups", "mp"), None)),
        check_vma=False,
    )
```

time: 149 us -> 129 us (0.87)
  Pallas kernels: 120 us -> 99.4 us
    pallas_call x3 -> x1, Pallas kernels: 120 us -> 99.4 us  [layer(): pl.pallas_call(functools.partial(layer_kernel, zs, slices), out_shape=[ja...]
    unnamed x7 -> x5, local copies, waits for them, and re-layouts: 4.94 us -> 5.9 us
where the time goes in v2:
time: 129 us
  Pallas kernels  99.4 us (77%)
  waiting for transfers between devices  9.83 us (8%)
  local copies, waits for them, and re-layouts  9.12 us (7%)
  starting transfers between devices  7.39 us (6%)
  matrix products  1.37 us (1%)
    pallas_call x1, Pallas kernels, layer(): pl.pallas_call(functools.partial(layer_kernel, zs, slices), out_shape=[ja...  99.4 us
    all_to_all x1, waiting for transfers between devices, local(): lax.all_to_all(sent.transpose(1, 0, 2), 'mp', split_axis=0, concat_axis=0...  9.83 us
    all_to_all x1, starting transfers between devices, local(): lax.all_to_all(sent.transpose(1, 0, 2), 'mp', split_axis=0, concat_axis=0...  7.39 us
    unnamed x5, local copies, waits for them, and re-layouts  5.9 us
  transfers between devices with their start and end apart: 1, of which 1 were waited for; matrix products, arithmetic and copies ran while one was open for 2% of the time, Pallas kernels for 0%

profile of v2, /device:TPU:0, one launch (start us, length us, event | category | flops | bytes accessed | tf_op | source)
XLA Modules:
  0.0 128.9 jit_solution(5005531201241790595)
XLA Ops:
  0.6 0.8 copy.51
  1.4 0.8 copy.50
  2.2 1.0 copy.49
  3.3 0.9 copy.39
  4.2 7.4 %all-to-all-start = ((bf16[16,16,768]{2,1,0:T(8,128)(2,1)}), bf16[16,16,768]{2,1,0:T(8,128)(2,1)S(1)}, u32[]{:S(2)}, u32[]{:S(2)}) async-start(bf16[16,16,768]{2,1,0:T(8,128)(2,1)} %copy.39), calls=%async_computation | async-start | bytes 786432 | tf_op jit(solution)/shard_map/all_to_all | solution.py:308
  11.6 0.1 ge.12
  11.7 0.8 reduce-window.8
  12.5 1.2 dynamic_slice.3.refs_0_
  13.7 0.1 convert_reduce_fusion
  13.8 0.1 fusion.7
  13.9 9.8 %all-to-all-done = bf16[16,16,768]{2,1,0:T(8,128)(2,1)S(1)} async-done(((bf16[16,16,768]{2,1,0:T(8,128)(2,1)}), bf16[16,16,768]{2,1,0:T(8,128)(2,1)S(1)}, u32[]{:S(2)}, u32[]{:S(2)}) %all-to-all-start) | async-done | bytes 393248 | tf_op jit(solution)/shard_map/all_to_all | solution.py:308
  23.8 0.1 reshape_reshape.11
  23.9 0.6 fusion.26
  24.5 0.8 convolution_convert_fusion
  25.3 0.8 copy.48.refs_1_
  26.2 99.4 %layer.1 = (bf16[16,8192]{1,0:T(8,128)(2,1)}, bf16[16,8192]{1,0:T(8,128)(2,1)}) custom-call(s32[6]{0:T(128)} %dynamic_slice.3.refs_0_, bf16[256,512]{1,0:T(8,128)(2,1)} %copy.48.refs_1_, bf16[16,8192]{1,0:T(8,128)(2,1)} %refs_2_.1, f32[2,8192]{1,0:T(2,128)} %refs_3_.1, bf16[512,8192]{1,0:T(8,128)(2,1)} %refs_4_.1, bf16[8192,768]{1,0:T(8,128)(2,1)} %refs_5_.1, ...), custom_call_target="tpu_custom_call" | custom-call | tf_op jit(solution)/shard_map/layer/pallas_call | solution.py:226
  125.6 1.7 %copy.68 = bf16[16,8192]{1,0:T(8,128)(2,1)} copy(bf16[16,8192]{1,0:T(8,128)(2,1)} %get-tuple-element.8) | data formatting | bytes 524288
  127.2 1.7 %copy.69 = bf16[16,8192]{1,0:T(8,128)(2,1)} copy(bf16[16,8192]{1,0:T(8,128)(2,1)} %get-tuple-element.9) | data formatting | bytes 524288
  (7 shorter events, 0.2 us)
Async XLA Ops:
  4.2 19.6 %all-to-all-start = ((bf16[16,16,768]{2,1,0:T(8,128)(2,1)}), bf16[16,16,768]{2,1,0:T(8,128)(2,1)S(1)}, u32[]{:S(2)}, u32[]{:S(2)}) async-start(bf16[16,16,768]{2,1,0:T(8,128)(2,1)} %copy.39), calls=%async_computation | async-start | bytes 786432 | tf_op jit(solution)/shard_map/all_to_all | solution.py:308

commit v3 on v2

--- a/solution.py
+++ b/solution.py
@@ -3,7 +3,6 @@
 
 import jax
 import jax.numpy as jnp
-import numpy as np
 from jax import lax
 from jax.experimental import pallas as pl
 from jax.experimental.pallas import tpu as pltpu
@@ -31,13 +30,17 @@
 
 
 def layer_kernel(zs, slices, *refs):
-    (which, a_ref, res_ref, gain_ref, w_hbm, gate_hbm, up_hbm, down_hbm, stream_ref, mixed_ref,
-     w, gate, up, part, from_core, pair, from_y, quad, from_z, whole, gained, square, acc, hidden,
+    (seq_lens, table, q_ref, k_ref, v_ref, res_ref, gain_ref, w_hbm, gate_hbm, up_hbm, down_hbm,
+     both_ref, packed, got, a_ref, ps, pr, w, gate, up, part, from_core, pair, from_y, quad, from_z, whole, gained, square, acc, hidden,
      w_sem, gate_sem, up_sem, cs, cr, ys, yr, zsend, zrecv, gzs, gzr, gys, gyr, gcs, gcr) = refs
     core, y, z, dev = place(zs)
     n, half, cw = from_core.shape
     rows = 2 * half
     tok = half // 2 // zs
+    mp = 4 * zs
+    q_width = packed.shape[2] - 2 * HEAD_SIZE
+    me = lax.axis_index("mp")
+    stream_ref, mixed_ref = both_ref.at[0], both_ref.at[1]
 
     def columns(j):
         return pl.ds(pl.multiple_of(j * cw, cw), cw)
@@ -83,21 +86,78 @@
         mine = whole.at[j, core]
         return remote(mine, mine, gcs.at[j], gcr.at[j], dev(z, y, 1 - core))
 
+    def head_copy(d):
+        to = lax.rem(me + d, mp)
+        return remote(packed.at[to], got.at[core, y, z], ps.at[d], pr.at[d], {"mp": to})
+
+    barrier = pltpu.get_barrier_semaphore()
+
+    @pl.loop(1, mp)
+    def _(d):
+        pl.semaphore_signal(
+            barrier, inc=1, device_id={"mp": lax.rem(me + d, mp)}, device_id_type=MESH
+        )
+
+    heads_kv = k_ref.shape[1] // HEAD_SIZE
+    per_group = QUERY_HEADS // heads_kv
+    local_heads = q_width // HEAD_SIZE
+    for to in range(mp):
+        head = to * local_heads // per_group
+        cols = slice(head * HEAD_SIZE, (head + 1) * HEAD_SIZE)
+        packed[to, :, :q_width] = q_ref[:, to * q_width : (to + 1) * q_width]
+        packed[to, :, q_width : q_width + HEAD_SIZE] = k_ref[:, cols]
+        packed[to, :, q_width + HEAD_SIZE :] = v_ref[:, cols]
+    got[core, y, z] = packed[me]
+    pl.semaphore_wait(barrier, mp - 1)
+
+    @pl.loop(1, mp)
+    def _(d):
+        head_copy(d).start()
+
     @pl.loop(0, n)
     def _(j):
         w_copy(j, True).start()
-
-    barrier = pltpu.get_barrier_semaphore()
-    partners = [dev(z, y, 1 - core), dev(z, 1 - y, core)]
-    partners += [dev(lax.rem(z + d, zs), y, core) for d in range(1, zs)]
-    for to in partners:
-        pl.semaphore_signal(barrier, inc=1, device_id=to, device_id_type=MESH)
-    pl.semaphore_wait(barrier, len(partners))
 
     @pl.loop(0, n)
     def _(j):
         gate_copy(j).start()
         up_copy(j).start()
+
+    def position(at):
+        token, z_at = at & (tok - 1), (at // tok) & (zs - 1)
+        y_at, core_at = (at // (tok * zs)) & 1, at // (tok * zs * 2)
+        return ((z_at * 2 + y_at) * 2 + core_at) * tok + token
+
+    query_pos = position(lax.broadcasted_iota(jnp.int32, (rows, 1), 0))
+    key_pos = position(lax.broadcasted_iota(jnp.int32, (1, rows), 1))
+    begin = jnp.zeros((rows, 1), jnp.int32)
+    end = 0
+    for k in range(seq_lens.shape[0]):
+        end = end + seq_lens[k]
+        begin = jnp.where(query_pos >= end, end, begin)
+    visible = (key_pos >= begin) & (key_pos <= query_pos)
+
+    @pl.loop(1, mp)
+    def _(d):
+        head_copy(d).wait_recv()
+
+    keys = got[:, :, :, :, q_width : q_width + HEAD_SIZE].reshape(rows, HEAD_SIZE)
+    vals = got[:, :, :, :, q_width + HEAD_SIZE :].reshape(rows, HEAD_SIZE)
+    for h in range(local_heads):
+        cols = slice(h * HEAD_SIZE, (h + 1) * HEAD_SIZE)
+        heads = got[:, :, :, :, cols].reshape(rows, HEAD_SIZE)
+        scores = lax.dot_general(
+            heads, keys, (((1,), (1,)), ((), ())), preferred_element_type=F32
+        ) * (1.0 / math.sqrt(HEAD_SIZE))
+        masked = jnp.where(visible, scores, -1e30)
+        highest = jnp.max(masked, axis=1, keepdims=True)
+        expo = jnp.where(visible, jnp.exp(masked - highest), 0.0)
+        probs = (expo / jnp.sum(expo, axis=1, keepdims=True)).astype(BF16)
+        a_ref[:, cols] = jnp.dot(probs, vals, preferred_element_type=F32).astype(BF16)
+
+    @pl.loop(1, mp)
+    def _(d):
+        head_copy(d).wait_send()
 
     square[...] = jnp.zeros_like(square)
     acc[...] = jnp.zeros_like(acc)
@@ -169,7 +229,7 @@
         for s in range(slices):
             cols = slice(s * SLICE, (s + 1) * SLICE)
             both = jnp.concatenate([gate[j, :, cols], up[j, :, cols]], axis=1)
-            acc[s] += jnp.dot(gained[which[s]], both, preferred_element_type=F32)
+            acc[s] += jnp.dot(gained[table[me * slices + s]], both, preferred_element_type=F32)
 
     def send_waits(j):
         core_copy(j).wait_send()
@@ -214,9 +274,13 @@
         send_waits(j)
 
 
-def layer(which, context, tokens, gain, out_weight, gate_weight, up_weight, down_weight, zs):
-    rows, depth = context.shape
+def layer(seq_lens, table, queries, keys, vals, tokens, gain, out_weight, gate_weight, up_weight,
+          down_weight, zs):
     tok, width = tokens.shape
+    depth = out_weight.shape[0]
+    mp = 4 * zs
+    rows = tok * mp
+    assert tok & (tok - 1) == 0 and zs & (zs - 1) == 0
     units = down_weight.shape[0]
     slices = units // SLICE
     n, cw, half = CHUNKS, width // CHUNKS, rows // 2
@@ -225,10 +289,14 @@
     hbm = pl.BlockSpec(memory_space=pl.ANY)
     return pl.pallas_call(
         functools.partial(layer_kernel, zs, slices),
-        out_shape=[jax.ShapeDtypeStruct((tok, width), BF16)] * 2,
-        in_specs=[pl.BlockSpec(memory_space=pltpu.SMEM)] + [vmem] * 3 + [hbm] * 4,
-        out_specs=[vmem] * 2,
+        out_shape=jax.ShapeDtypeStruct((2, tok, width), BF16),
+        in_specs=[pl.BlockSpec(memory_space=pltpu.SMEM)] * 2 + [vmem] * 5 + [hbm] * 4,
+        out_specs=vmem,
         scratch_shapes=[
+            pltpu.VMEM((mp, tok, depth + 2 * HEAD_SIZE), BF16),
+            pltpu.VMEM((2, 2, zs, tok, depth + 2 * HEAD_SIZE), BF16),
+            pltpu.VMEM((rows, depth), BF16),
+            dma((mp,)), dma((mp,)),
             pltpu.VMEM((n, max(depth, units), cw), BF16),
             pltpu.VMEM((n, cw, units), BF16),
             pltpu.VMEM((n, cw, units), BF16),
@@ -251,76 +319,16 @@
             collective_id=0, has_side_effects=True, vmem_limit_bytes=60 << 20
         ),
         name="layer",
-    )(which, context, tokens, gain, out_weight, gate_weight, up_weight, down_weight)
-
-
-def attention(query_rows, key_cols, value_cols, query_pos, seq_lens, local_heads):
-    count = query_rows.shape[0]
-    seq_ends = jnp.cumsum(seq_lens)
-    key_pos = jnp.arange(count, dtype=jnp.int32)
-
-    def segment_of(positions):
-        return jnp.sum((positions[:, None] >= seq_ends[None, :]).astype(jnp.int32), axis=1)
-
-    visible = (segment_of(query_pos)[:, None] == segment_of(key_pos)[None, :]) & (
-        key_pos[None, :] <= query_pos[:, None]
-    )
-    scores = jnp.einsum(
-        "thd,sd->hts",
-        query_rows.reshape(count, local_heads, HEAD_SIZE),
-        key_cols,
-        preferred_element_type=F32,
-    ) * (1.0 / math.sqrt(HEAD_SIZE))
-    masked = jnp.where(visible[None], scores, -1e30)
-    highest = jnp.max(masked, axis=-1, keepdims=True)
-    expo = jnp.where(visible[None], jnp.exp(masked - highest), 0.0)
-    probs = (expo / jnp.sum(expo, axis=-1, keepdims=True)).astype(BF16)
-    return (
-        jnp.einsum("hts,sd->thd", probs, value_cols, preferred_element_type=F32)
-        .astype(BF16)
-        .reshape(count, local_heads * HEAD_SIZE)
-    )
+    )(seq_lens, table, queries, keys, vals, tokens, gain, out_weight, gate_weight, up_weight, down_weight)
 
 
 def local(tokens, queries, key_proj, values, seq_lens, out_weight, ffn_gain, gate_weight, up_weight,
           down_weight, slice_table):
-    tok = tokens.shape[0]
-    mp = lax.axis_size("mp")
-    zs = mp // 4
-    count = tok * mp
-    me = lax.axis_index("mp")
-    heads_kv = key_proj.shape[1] // HEAD_SIZE
-    per_group = QUERY_HEADS // heads_kv
-    local_heads = QUERY_HEADS // mp
-
-    kv_heads = np.arange(mp) * local_heads // per_group
-    repeat = mp // heads_kv
-    assert (kv_heads == np.arange(mp) // repeat).all()
-
-    def for_devices(rows):
-        return jnp.repeat(rows.reshape(tok, heads_kv, 1, HEAD_SIZE), repeat, axis=2).reshape(
-            tok, mp, HEAD_SIZE
-        )
-
-    sent = jnp.concatenate(
-        [queries.reshape(tok, mp, -1), for_devices(key_proj), for_devices(values)], axis=2
+    both = layer(
+        seq_lens, slice_table, queries, key_proj, values, tokens, ffn_gain, out_weight, gate_weight,
+        up_weight, down_weight, lax.axis_size("mp") // 4
     )
-    got = lax.all_to_all(sent.transpose(1, 0, 2), "mp", split_axis=0, concat_axis=0, tiled=True)
-    q_width = local_heads * HEAD_SIZE
-    key_cols = got[:, :, q_width : q_width + HEAD_SIZE].reshape(count, HEAD_SIZE)
-    value_cols = got[:, :, q_width + HEAD_SIZE :].reshape(count, HEAD_SIZE)
-
-    def reorder(rows):
-        return rows.reshape(zs, 2, 2, tok, -1).transpose(2, 1, 0, 3, 4)
-
-    query_rows = reorder(got[:, :, :q_width]).reshape(count, q_width)
-    query_pos = reorder(jnp.arange(count, dtype=jnp.int32)).reshape(count)
-    context = attention(query_rows, key_cols, value_cols, query_pos, seq_lens, local_heads)
-    slices = gate_weight.shape[1] // SLICE
-    which = lax.dynamic_slice_in_dim(slice_table, me * slices, slices)
-    stream, mixed = layer(
-        which, context, tokens, ffn_gain, out_weight, gate_weight, up_weight, down_weight, zs
-    )
+    stream, mixed = both[0], both[1]
     return (stream, mixed)
 
 

time: 129 us -> 117 us (0.907)
  Pallas kernels: 99.4 us -> 115 us
  waiting for transfers between devices: 9.83 us -> 0 us
  starting transfers between devices: 7.39 us -> 0 us
  local copies, waits for them, and re-layouts: 9.12 us -> 1.85 us
  matrix products: 1.37 us -> 0 us
    pallas_call x1, Pallas kernels: 99.4 us -> 115 us  [layer(): pl.pallas_call(functools.partial(layer_kernel, zs, slices), out_shape=jax...]
    all_to_all x1 -> x0, waiting for transfers between devices: 9.83 us -> none  [local(): lax.all_to_all(sent.transpose(1, 0, 2), 'mp', split_axis=0, concat_axis=0...]
    all_to_all x1 -> x0, starting transfers between devices: 7.39 us -> none  [local(): lax.all_to_all(sent.transpose(1, 0, 2), 'mp', split_axis=0, concat_axis=0...]
    unnamed x5 -> x0, local copies, waits for them, and re-layouts: 5.9 us -> none
    squeeze x0 -> x1, local copies, waits for them, and re-layouts: none -> 1.85 us  [local(): stream, mixed = (both[0], both[1])]
  transfers between devices with their start and end apart: 1 -> 0, of which waited for: 1 -> 0; matrix products, arithmetic and copies ran while one was open for 2% -> 0% of each run, Pallas kernels for 0% -> 0%
where the time goes in v3:
time: 117 us
  Pallas kernels  115 us (98%)
  local copies, waits for them, and re-layouts  1.85 us (2%)
    pallas_call x1, Pallas kernels, layer(): pl.pallas_call(functools.partial(layer_kernel, zs, slices), out_shape=jax...  115 us

profile of v3, /device:TPU:0, one launch (start us, length us, event | category | flops | bytes accessed | tf_op | source)
XLA Modules:
  0.0 117.1 jit_solution(6346209727969311824)
XLA Ops:
  0.6 114.6 %layer.1 = bf16[2,16,8192]{2,1,0:T(8,128)(2,1)} custom-call(s32[6]{0:T(128)} %refs_0_.1, s32[96]{0:T(128)} %refs_1_.1, bf16[16,8192]{1,0:T(8,128)(2,1)} %refs_2_.1, bf16[16,1024]{1,0:T(8,128)(2,1)} %refs_3_.1, bf16[16,1024]{1,0:T(8,128)(2,1)} %refs_4_.1, bf16[16,8192]{1,0:T(8,128)(2,1)} %refs_5_.1, f32[2,8192]{1,0:T(2,128)} %refs_6_.1, ...), custom_call_target="tpu_custom_call" | custom-call | tf_op jit(solution)/shard_map/layer/pallas_call | solution.py:290
  115.3 1.9 %slice_bitcast_fusion = (bf16[16,8192]{1,0:T(8,128)(2,1)}, bf16[16,8192]{1,0:T(8,128)(2,1)}) fusion(bf16[2,16,8192]{2,1,0:T(8,128)(2,1)} %layer.1), kind=kLoop, calls=%fused_computation | loop fusion | bytes 1048576 | tf_op jit(solution)/shard_map/squeeze | solution.py:331

commit v4 on v3

--- a/solution.py
+++ b/solution.py
@@ -90,6 +90,10 @@
         to = lax.rem(me + d, mp)
         return remote(packed.at[to], got.at[core, y, z], ps.at[d], pr.at[d], {"mp": to})
 
+    @pl.loop(0, n)
+    def _(j):
+        w_copy(j, True).start()
+
     barrier = pltpu.get_barrier_semaphore()
 
     @pl.loop(1, mp)
@@ -110,13 +114,9 @@
     got[core, y, z] = packed[me]
     pl.semaphore_wait(barrier, mp - 1)
 
-    @pl.loop(1, mp)
-    def _(d):
-        head_copy(d).start()
-
-    @pl.loop(0, n)
-    def _(j):
-        w_copy(j, True).start()
+    @pl.loop(0, mp - 1)
+    def _(i):
+        head_copy(lax.rem(i + mp // 2 - 1, mp - 1) + 1).start()
 
     @pl.loop(0, n)
     def _(j):

time: 117 us -> 118 us (level)
  no operation moved by 1% of the time
where the time goes in v4:
time: 118 us; the launch traced here: 117 us
  Pallas kernels  115 us (97%)
  local copies, waits for them, and re-layouts  1.85 us (2%)
    pallas_call x1, Pallas kernels, layer(): pl.pallas_call(functools.partial(layer_kernel, zs, slices), out_shape=jax...  115 us

profile of v4, /device:TPU:0, one launch (start us, length us, event | category | flops | bytes accessed | tf_op | source)
XLA Modules:
  0.0 117.4 jit_solution(6501680507573614600)
XLA Ops:
  0.6 114.9 %layer.1 = bf16[2,16,8192]{2,1,0:T(8,128)(2,1)} custom-call(s32[6]{0:T(128)} %refs_0_.1, s32[96]{0:T(128)} %refs_1_.1, bf16[16,8192]{1,0:T(8,128)(2,1)} %refs_2_.1, bf16[16,1024]{1,0:T(8,128)(2,1)} %refs_3_.1, bf16[16,1024]{1,0:T(8,128)(2,1)} %refs_4_.1, bf16[16,8192]{1,0:T(8,128)(2,1)} %refs_5_.1, f32[2,8192]{1,0:T(2,128)} %refs_6_.1, ...), custom_call_target="tpu_custom_call" | custom-call | tf_op jit(solution)/shard_map/layer/pallas_call | solution.py:290
  115.5 1.9 %slice_bitcast_fusion = (bf16[16,8192]{1,0:T(8,128)(2,1)}, bf16[16,8192]{1,0:T(8,128)(2,1)}) fusion(bf16[2,16,8192]{2,1,0:T(8,128)(2,1)} %layer.1), kind=kLoop, calls=%fused_computation | loop fusion | bytes 1048576 | tf_op jit(solution)/shard_map/squeeze | solution.py:331
